TPU v7x, 128 devices: a whole 4x4x4 slice. The times are simulated.
128 devices in a mesh: gene: 8 (over y, x_lo), bin: 16 (over z, x_hi, core).
Axes of the slice: x: 4 (x_hi: 2, x_lo: 2; x = x_hi * 2 + x_lo), y: 4, z: 4, core: 2. Of those that a mesh axis runs over, the one named last changes fastest.
Arguments:
- counts: bfloat16 [49152, 18432], P('bin', 'gene'), may hold values from 2 to 80
- factors: float32 [49152, 256], P('bin'), may hold values from 0.01 to 1
- loadings: float32 [256, 18432], P(None, 'gene'), may hold values from 0.01 to 1
- position: int32 [49152], P('bin'), may hold values from 0 to 49151, as said below
- edge_codes: int32 [192, 256], P('bin'), may hold values from 1 to 15
Outputs:
- factors_new: float32 [49152, 256], P('bin')
- loadings_new: float32 [256, 18432], P(None, 'gene')
Inputs may be any that keep to these rules, and one draw needn't show every extreme that they name: Each grid position is named by exactly one barcode. The barcodes of one index s of bin (rows s * 3072 on) fall in 16 aligned groups of 192; group t holds positions in grid rows t * 12 to (t + 1) * 12 - 1, 192 from every such index.
All inputs are finite; a program needn't handle non-finite values.
Results may differ from a plain program's by a relative error of at most 0.0003.
Values sent between devices are 32-bit elements; how exact they have to be, the bound alone decides.
A program may use at most 128 MiB of HBM per device.

v0:
```python
import functools

import jax
import jax.numpy as jnp
from jax import lax
from jax.experimental import pallas as pl
from jax.experimental.pallas import tpu as pltpu
from jax.sharding import PartitionSpec as P

K = 256
G = 18432


def passed_along(block, axis, distance):
    devices = range(lax.axis_size(axis))
    route = [(i - distance, i) for i in devices if i - distance in devices]
    return lax.ppermute(block, axis, route)


def neighbour_sum(values, from_above, from_below):
    upper = jnp.concatenate([from_above[None], values[:-1]], 0)
    lower = jnp.concatenate([values[1:], from_below[None]], 0)
    beside = jnp.pad(values[:, 1:], ((0, 0), (0, 1), (0, 0))) + jnp.pad(
        values[:, :-1], ((0, 0), (1, 0), (0, 0))
    )
    return beside + 0.5 * (lower + upper)


def neighbour_first(values, from_above, from_below):
    upper = jnp.concatenate([from_above[:, None], values[:, :-1]], 1)
    lower = jnp.concatenate([values[:, 1:], from_below[:, None]], 1)
    beside = jnp.pad(values[:, :, 1:], ((0, 0), (0, 0), (0, 1))) + jnp.pad(
        values[:, :, :-1], ((0, 0), (0, 0), (1, 0))
    )
    return beside + 0.5 * (lower + upper)


def gray(value):
    return value + (value // 2) * (1 - 2 * (value % 2))


def gene_at_place(place, count):
    wide = 1 - ((place + count - 1) % count) // (count // 2)
    row = wide * (place - 1) + (1 - wide) * ((count - place) % count)
    return 2 * row + wide


def gene_place(index, count):
    row, wide = index // 2, index % 2
    return wide * (1 + row) + (1 - wide) * ((count - row) % count)


def bin_at_place(place, count):
    plane, step = place // 4, place % 4
    turned = step + (plane % 2) * (3 - 2 * step)
    return plane * 4 + gray(turned)


def bin_place(index, count):
    plane = index // 4
    turned = gray(index % 4)
    return plane * 4 + turned + (plane % 2) * (3 - 2 * turned)


RINGS = {"gene": (gene_at_place, gene_place), "bin": (bin_at_place, bin_place)}


def ring_peers(axis, count):
    at_place, place_of = RINGS[axis]
    place = place_of(lax.axis_index(axis), count)
    return place, (lambda shift: at_place((place + shift + count) % count, count))


def enter(axis, peers):
    barrier = pltpu.get_barrier_semaphore()
    for peer in peers:
        pl.semaphore_signal(barrier, inc=1, device_id={axis: peer},
                            device_id_type=pl.DeviceIdType.MESH)
    pl.semaphore_wait(barrier, len(peers))


def gather_kernel(axis, count, x_ref, out_ref, send_sem, recv_sem):
    place, member = ring_peers(axis, count)
    ahead, behind = member(1), member(-1)
    half = x_ref.shape[0] // 2
    enter(axis, (ahead, behind))
    out_ref[member(0)] = x_ref[...]

    def copy(step, way):
        rows = pl.ds(way * half, half)
        origin = member(-step) if way == 0 else member(step)
        src = x_ref.at[rows] if step == 0 else out_ref.at[origin, rows]
        return pltpu.make_async_remote_copy(
            src_ref=src,
            dst_ref=out_ref.at[origin, rows],
            send_sem=send_sem.at[way, step],
            recv_sem=recv_sem.at[way, step],
            device_id={axis: ahead if way == 0 else behind},
            device_id_type=pl.DeviceIdType.MESH,
        )

    for step in range(count - 1):
        for way in (0, 1):
            if step >= 1:
                copy(step - 1, way).wait_recv()
            copy(step, way).start()
    for way in (0, 1):
        copy(count - 2, way).wait_recv()
    for step in range(count - 1):
        for way in (0, 1):
            copy(step, way).wait_send()


def ring_gather(x, axis, collective_id):
    count = lax.axis_size(axis)
    return pl.pallas_call(
        functools.partial(gather_kernel, axis, count),
        out_shape=jax.ShapeDtypeStruct((count,) + x.shape, x.dtype),
        in_specs=[pl.BlockSpec(memory_space=pltpu.VMEM)],
        out_specs=pl.BlockSpec(memory_space=pltpu.VMEM),
        scratch_shapes=[
            pltpu.SemaphoreType.DMA((2, count - 1)),
            pltpu.SemaphoreType.DMA((2, count - 1)),
        ],
        compiler_params=pltpu.CompilerParams(
            collective_id=collective_id, has_side_effects=True
        ),
    )(x)


def scatter_kernel(axis, count, x_ref, out_ref, got, sent, send_sem, recv_sem):
    place, member = ring_peers(axis, count)
    ahead, behind = member(1), member(-1)
    half = x_ref.shape[2] // 2
    enter(axis, (ahead, behind))

    def copy(step, way):
        lanes = pl.ds(way * half, half)
        if step == 0:
            source = x_ref.at[member(-1) if way == 0 else member(1), :, lanes]
        else:
            source = sent.at[way, step]
        return pltpu.make_async_remote_copy(
            src_ref=source,
            dst_ref=got.at[way, step],
            send_sem=send_sem.at[way, step],
            recv_sem=recv_sem.at[way, step],
            device_id={axis: ahead if way == 0 else behind},
            device_id_type=pl.DeviceIdType.MESH,
        )

    for step in range(count - 1):
        for way in (0, 1):
            if step >= 1:
                lanes = pl.ds(way * half, half)
                owner = member(-step - 1) if way == 0 else member(step + 1)
                copy(step - 1, way).wait_recv()
                sent[way, step] = got[way, step - 1] + x_ref[owner, :, lanes]
            copy(step, way).start()
    for way in (0, 1):
        lanes = pl.ds(way * half, half)
        copy(count - 2, way).wait_recv()
        out_ref[:, lanes] = got[way, count - 2] + x_ref[member(0), :, lanes]
    for step in range(count - 1):
        for way in (0, 1):
            copy(step, way).wait_send()


def ring_scatter(x, axis, collective_id):
    count, rows, lanes = x.shape
    return pl.pallas_call(
        functools.partial(scatter_kernel, axis, count),
        out_shape=jax.ShapeDtypeStruct((rows, lanes), x.dtype),
        in_specs=[pl.BlockSpec(memory_space=pltpu.VMEM)],
        out_specs=pl.BlockSpec(memory_space=pltpu.VMEM),
        scratch_shapes=[
            pltpu.VMEM((2, count - 1, rows, lanes // 2), x.dtype),
            pltpu.VMEM((2, count - 1, rows, lanes // 2), x.dtype),
            pltpu.SemaphoreType.DMA((2, count - 1)),
            pltpu.SemaphoreType.DMA((2, count - 1)),
        ],
        compiler_params=pltpu.CompilerParams(
            collective_id=collective_id, has_side_effects=True
        ),
    )(x)


def greet_all(axis, me, count):
    barrier = pltpu.get_barrier_semaphore()
    for shift in range(1, count):
        pl.semaphore_signal(barrier, inc=1, device_id={axis: (me + shift) % count},
                            device_id_type=pl.DeviceIdType.MESH)
    pl.semaphore_wait(barrier, count - 1)


def exchange_kernel(axis, count, summed, x_ref, out_ref, *rest):
    if summed:
        got, send_sem, recv_sem = rest
    else:
        got, (send_sem, recv_sem) = out_ref, rest
    me = lax.axis_index(axis)
    greet_all(axis, me, count)

    def copy(shift):
        target = (me + shift) % count
        return pltpu.make_async_remote_copy(
            src_ref=x_ref.at[target] if summed else x_ref,
            dst_ref=got.at[me],
            send_sem=send_sem.at[shift],
            recv_sem=recv_sem.at[me],
            device_id={axis: target},
            device_id_type=pl.DeviceIdType.MESH,
        )

    def arrival(shift):
        origin = (me + count - shift) % count
        return pltpu.make_async_remote_copy(
            src_ref=x_ref.at[origin] if summed else x_ref,
            dst_ref=got.at[origin],
            send_sem=send_sem.at[shift],
            recv_sem=recv_sem.at[origin],
            device_id={axis: origin},
            device_id_type=pl.DeviceIdType.MESH,
        )

    for shift in range(1, count):
        copy(shift).start()
    if summed:
        total = x_ref[me]
        for shift in range(1, count):
            arrival(shift).wait_recv()
            total = total + got[(me + count - shift) % count]
        out_ref[...] = total
    else:
        out_ref[me] = x_ref[...]
        for shift in range(1, count):
            arrival(shift).wait_recv()
    for shift in range(1, count):
        copy(shift).wait_send()


def exchange(x, axis, collective_id, summed):
    count = lax.axis_size(axis)
    if summed:
        out_shape = x.shape[1:]
        scratch = [pltpu.VMEM(x.shape, x.dtype)]
    else:
        out_shape = (count,) + x.shape
        scratch = []
    return pl.pallas_call(
        functools.partial(exchange_kernel, axis, count, summed),
        out_shape=jax.ShapeDtypeStruct(out_shape, x.dtype),
        in_specs=[pl.BlockSpec(memory_space=pltpu.VMEM)],
        out_specs=pl.BlockSpec(memory_space=pltpu.VMEM),
        scratch_shapes=scratch + [
            pltpu.SemaphoreType.DMA((count,)),
            pltpu.SemaphoreType.DMA((count,)),
        ],
        compiler_params=pltpu.CompilerParams(
            collective_id=collective_id, has_side_effects=True
        ),
    )(x)


def loadings_kernel(count, cross_ref, gram_ref, load_ref, out_ref, got, got_gram, sem_a, sem_b, sem_c, sem_d):
    me = lax.axis_index("bin")
    greet_all("bin", me, count)

    def remote(src, dst, send, recv, shift, index, peer):
        return pltpu.make_async_remote_copy(
            src_ref=src.at[index],
            dst_ref=dst.at[index],
            send_sem=send.at[shift],
            recv_sem=recv.at[index],
            device_id={"bin": peer},
            device_id_type=pl.DeviceIdType.MESH,
        )

    def partial_copies(shift):
        target = (me + shift) % count
        return (
            pltpu.make_async_remote_copy(
                src_ref=cross_ref.at[target], dst_ref=got.at[me], send_sem=sem_a.at[0, shift],
                recv_sem=sem_b.at[0, me], device_id={"bin": target},
                device_id_type=pl.DeviceIdType.MESH,
            ),
            pltpu.make_async_remote_copy(
                src_ref=gram_ref.at[target], dst_ref=got_gram.at[me], send_sem=sem_a.at[1, shift],
                recv_sem=sem_b.at[1, me], device_id={"bin": target},
                device_id_type=pl.DeviceIdType.MESH,
            ),
        )

    def partial_arrivals(shift):
        origin = (me + count - shift) % count
        return (
            pltpu.make_async_remote_copy(
                src_ref=cross_ref.at[origin], dst_ref=got.at[origin], send_sem=sem_a.at[0, shift],
                recv_sem=sem_b.at[0, origin], device_id={"bin": origin},
                device_id_type=pl.DeviceIdType.MESH,
            ),
            pltpu.make_async_remote_copy(
                src_ref=gram_ref.at[origin], dst_ref=got_gram.at[origin], send_sem=sem_a.at[1, shift],
                recv_sem=sem_b.at[1, origin], device_id={"bin": origin},
                device_id_type=pl.DeviceIdType.MESH,
            ),
        )

    def result_copy(shift):
        target = (me + shift) % count
        return remote(out_ref, out_ref, sem_c, sem_d, shift, me, target)

    def result_arrival(shift):
        origin = (me + count - shift) % count
        return remote(out_ref, out_ref, sem_c, sem_d, shift, origin, origin)

    for shift in range(1, count):
        for copy in partial_copies(shift):
            copy.start()
    cross = cross_ref[me]
    fac_gram = gram_ref[me]
    for shift in range(1, count):
        origin = (me + count - shift) % count
        for copy in partial_arrivals(shift):
            copy.wait_recv()
        cross = cross + got[origin]
        fac_gram = fac_gram + got_gram[origin]
    rows = cross.shape[0]
    own = load_ref[pl.ds(pl.multiple_of(me * rows, rows), rows), :]
    denom = jnp.dot(
        fac_gram, load_ref[...], precision=lax.Precision.HIGHEST,
        preferred_element_type=jnp.float32,
    )
    out_ref[me] = own * cross / denom
    for shift in range(1, count):
        for copy in partial_copies(shift):
            copy.wait_send()
    for shift in range(1, count):
        result_copy(shift).start()
    for shift in range(1, count):
        result_arrival(shift).wait_recv()
    for shift in range(1, count):
        result_copy(shift).wait_send()


def loadings_update(cross_parts, gram_parts, loadings, collective_id):
    count, rows, genes = cross_parts.shape
    vmem = pl.BlockSpec(memory_space=pltpu.VMEM)
    return pl.pallas_call(
        functools.partial(loadings_kernel, count),
        out_shape=jax.ShapeDtypeStruct((count, rows, genes), loadings.dtype),
        in_specs=[vmem, vmem, vmem],
        out_specs=vmem,
        scratch_shapes=[
            pltpu.VMEM(cross_parts.shape, cross_parts.dtype),
            pltpu.VMEM(gram_parts.shape, gram_parts.dtype),
            pltpu.SemaphoreType.DMA((2, count)),
            pltpu.SemaphoreType.DMA((2, count)),
            pltpu.SemaphoreType.DMA((count,)),
            pltpu.SemaphoreType.DMA((count,)),
        ],
        compiler_params=pltpu.CompilerParams(
            collective_id=collective_id, has_side_effects=True
        ),
    )(cross_parts, gram_parts, loadings)


def split_three(values):
    high = lax.reduce_precision(values, exponent_bits=8, mantissa_bits=7)
    rest = values - high
    mid = lax.reduce_precision(rest, exponent_bits=8, mantissa_bits=7)
    low = rest - mid
    return jnp.concatenate([high, mid, low], 1).astype(jnp.bfloat16)


def join_three(parts, width):
    return (parts[:, :width] + parts[:, width : 2 * width]) + parts[:, 2 * width :]


def stencil_term(own, position, edge_codes):
    bin_count = lax.axis_size("bin")
    row_count, width = own.shape
    group_size = row_count // bin_count
    grid_rows, grid_cols = edge_codes.shape
    payload = jnp.concatenate([own, position.astype(jnp.float32)[:, None]], 1)
    got = lax.all_to_all(
        payload.reshape(bin_count, group_size, width + 1), "bin", 0, 0, tiled=True
    ).reshape(row_count, width + 1)
    tile_slot = got[:, width].astype(jnp.int32) - lax.axis_index("bin") * row_count
    cells = lax.broadcasted_iota(jnp.int32, (row_count, row_count), 1)
    onehot = (tile_slot[:, None] == cells).astype(jnp.bfloat16)
    placed = lax.dot_general(
        onehot, split_three(got[:, :width]), (((0,), (0,)), ((), ())),
        preferred_element_type=jnp.float32,
    )
    tile_rows = join_three(placed, width)
    cell_scale = edge_codes.astype(jnp.float32) / 8.0
    weighted = cell_scale[:, :, None] * tile_rows.reshape(grid_rows, grid_cols, width)
    rim_last, rim_first = (weighted[-1], weighted[0])
    upper_rows, upper_scale = passed_along((rim_last, cell_scale[-1]), "bin", 1)
    lower_rows, lower_scale = passed_along((rim_first, cell_scale[0]), "bin", -1)
    degree_grid = (
        cell_scale * neighbour_first(cell_scale[None], upper_scale[None], lower_scale[None])[0]
    )
    smooth_grid = cell_scale[:, :, None] * neighbour_sum(weighted, upper_rows, lower_rows)
    back = jnp.concatenate(
        [smooth_grid.reshape(row_count, width), degree_grid.reshape(row_count, 1)], 1
    )
    back_rows = join_three(
        jnp.dot(onehot, split_three(back), preferred_element_type=jnp.float32), width + 1
    )
    ret = lax.all_to_all(
        back_rows.reshape(bin_count, group_size, width + 1), "bin", 0, 0, tiled=True
    ).reshape(row_count, width + 1)
    return (ret[:, :width], ret[:, width])


def on_device(counts, factors, loadings, position, edge_codes):
    bin_count = lax.axis_size("bin")
    gene_count = lax.axis_size("gene")
    row_count, width_all = factors.shape
    width = width_all // gene_count
    k_rows = width_all // bin_count
    gene_at = lax.axis_index("gene")
    bin_at = lax.axis_index("bin")
    load_bf = loadings.astype(jnp.bfloat16)
    right_dims = (((1,), (1,)), ((), ()))
    numer_part = lax.dot_general(load_bf, counts, right_dims, preferred_element_type=jnp.float32)
    gram_part = lax.dot_general(load_bf, load_bf, right_dims, preferred_element_type=jnp.float32)
    both = jnp.concatenate([numer_part, gram_part], 1)
    both = lax.psum_scatter(
        both.reshape(gene_count, width, -1), "gene", scatter_dimension=0, tiled=True
    ).reshape(width, -1)
    numer_t, gram_rows = both[:, :row_count], both[:, row_count:]
    own = lax.dynamic_slice_in_dim(factors, gene_at * width, width, 1)
    smooth, degree = stencil_term(own, position, edge_codes)
    penalty = float(G * K) / 64.0
    own_t = own.T
    denom_t = (
        lax.dot_general(gram_rows, factors, right_dims, precision=lax.Precision.HIGHEST)
        + penalty * degree[None, :] * own_t
    )
    new_t = own_t * (numer_t + penalty * smooth.T) / denom_t
    factors_t = exchange(new_t, "gene", 0, False).reshape(width_all, row_count)
    factors_new = factors_t.T
    fac_bf_t = factors_t.astype(jnp.bfloat16)
    cross_part = jnp.dot(fac_bf_t, counts, preferred_element_type=jnp.float32)
    fgram_part = lax.dot_general(fac_bf_t, fac_bf_t, right_dims, preferred_element_type=jnp.float32)
    loadings_new = loadings_update(
        cross_part.reshape(bin_count, k_rows, -1),
        fgram_part.reshape(bin_count, k_rows, -1),
        loadings,
        2,
    ).reshape(width_all, -1)
    return (factors_new, loadings_new)


def solution(mesh):
    placed = (P("bin", "gene"), P("bin", None), P(None, "gene"), P("bin"), P("bin", None))
    return jax.shard_map(
        on_device,
        mesh=mesh,
        in_specs=placed,
        out_specs=(P("bin", None), P(None, "gene")),
        check_vma=False,
    )
```

profile of v0, /device:TPU:1, one launch (start us, length us, event | category | flops | bytes accessed | tf_op | source)
XLA Modules:
  0.0 281.1 jit_solution(4437988599628090535)
XLA Ops:
  7.2 0.0 copy-start
  7.2 0.9 convert_element_type.37
  8.0 0.1 concatenate.56
  8.1 1.0 copy-done
  9.1 1.6 constant_dynamic-slice_fusion
  10.7 1.8 copy.34
  12.5 1.0 concatenate.55
  13.6 1.1 pad_maximum_fusion.1
  14.7 1.2 copy.26
  15.8 9.3 %all-to-all-start = ((f32[16,192,33]{1,2,0:T(8,128)}), f32[16,192,33]{1,2,0:T(8,128)}, u32[]{:S(2)}, u32[]{:S(2)}) async-start(f32[16,192,33]{1,2,0:T(8,128)} %copy.26), calls=%async_computation.1 | async-start | bytes 1310720 | tf_op jit(solution)/shard_map/all_to_all | solution.py:386
  25.1 0.0 reduce-scatter.2.cloned.1.call-start
  25.2 0.0 copy-start.2
  25.2 0.9 fusion.38
  26.0 0.6 fusion.43
  26.7 2.0 collective-permute-start.2
  28.7 5.0 %collective-permute-start.3 = (f32[256]{0:T(256)}, f32[256]{0:T(256)}, u32[]{:S(2)}, u32[]{:S(2)}) collective-permute-start(f32[256]{0:T(256)} %bitcast.9), channel_id=1, source_target_pairs={{0,1},{1,2},{2,3},{3,4},{4,5},{5,6},{6,7},{7,8},{8,9},{9,10},{10,1... | collective-permute-start | bytes 3080 | tf_op jit(solution)/shard_map/ppermute | solution.py:17
  33.7 2.9 %fusion.17 = f32[256,256]{1,0:T(8,128)S(1)} fusion(f32[256,2304]{1,0:T(8,128)} %load_ref.1), kind=kOutput, calls=%fused_computation.24 | convolution fusion | flops 302579712 | bytes 2621440 | tf_op jit(solution)/shard_map/dot_general | solution.py:429
  36.6 10.7 %fusion.19 = f32[256,3072]{1,0:T(8,128)} fusion(bf16[3072,2304]{1,0:T(8,128)(2,1)} %param.5, f32[256,2304]{1,0:T(8,128)S(1)} %copy-done.2), kind=kOutput, calls=%fused_computation.26 | convolution fusion | flops 3624468480 | bytes 19660800 | tf_op jit(solution)/shard_map/dot_general | solution.py:428
  47.3 3.8 %pad_maximum_fusion = f32[256,3328]{1,0:T(8,128)} fusion(f32[256,256]{1,0:T(8,128)S(1)} %fusion.17, f32[256,3072]{1,0:T(8,128)} %fusion.19), kind=kLoop, calls=%fused_computation.9 | loop fusion | flops 851968 | bytes 6815744 | tf_op jit(solution)/shard_map/concatenate | solution.py:430
  51.2 0.0 reduce-scatter.2.cloned.1.call-update
  51.2 0.6 fusion.44
  51.8 0.7 fusion.42
  52.5 0.0 collective-permute-done.2
  52.5 0.0 collective-permute-done.3
  52.5 0.9 fusion.34
  53.3 0.6 copy.38
  54.0 0.0 all-to-all-done
  54.0 2.1 copy.27
  56.0 2.1 reshape.123
  58.1 0.9 fusion.35
  59.0 1.1 reduce-precision_convert_fusion.3
  60.1 7.5 %fusion.1 = f32[3072,96]{0,1:T(8,128)S(1)} fusion(s32[3072]{0:T(1024)S(1)} %bitcast.86, bf16[3072,32]{0,1:T(8,128)(2,1)S(1)} %get-tuple-element.12, bf16[3072,32]{0,1:T(8,128)(2,1)S(1)} %get-tuple-element.13, bf16[3072,32]{0,1:T(8,128)(2,1)S(1)} %get-tuple-element.11), kind=kOutput, calls=%fused_computation.2 | convolution fusion | flops 1823145984 | bytes 1781760 | tf_op jit(solution)/shard_map/dot_general | solution.py:392
  67.6 0.0 copy-done.5
  67.6 0.8 slice_add_fusion.2
  68.4 1.9 reshape.124
  70.3 1.1 broadcast_multiply_fusion
  71.5 1.9 collective-permute-start
  73.4 5.3 %collective-permute-start.1 = (f32[256,32]{0,1:T(8,128)S(1)}, f32[256,32]{0,1:T(8,128)S(1)}, u32[]{:S(2)}, u32[]{:S(2)}) collective-permute-start(f32[256,32]{0,1:T(8,128)S(1)} %bitcast.85), channel_id=1, source_target_pairs={{0,1},{1,2},{2,3},{3,4},{4,5},{5,6},{6,7},{7,8},{8,9},{9,10},{10,1... | collective-permute-start | bytes 98312 | tf_op jit(solution)/shard_map/ppermute | solution.py:17
  78.8 0.1 fusion.41
  78.9 0.2 fusion.39
  79.1 0.0 collective-permute-done
  79.1 1.2 collective-permute-done.1
  80.3 0.3 fusion.23
  80.6 0.2 copy.37
  80.9 0.8 constant_dynamic-update-slice_fusion
  81.7 1.6 dynamic-update-slice.1
  83.2 1.1 reduce-precision_convert_fusion.1
  84.4 8.1 %fusion = f32[3072,99]{0,1:T(8,128)S(1)} fusion(s32[3072]{0:T(1024)S(1)} %bitcast.87, bf16[3072,33]{0,1:T(8,128)(2,1)S(1)} %get-tuple-element.9, bf16[3072,33]{0,1:T(8,128)(2,1)S(1)} %get-tuple-element.10, bf16[3072,33]{0,1:T(8,128)(2,1)S(1)} %get-tuple-element.8), kind=kOutput, calls=%fused_computation.1 | convolution fusion | flops 1879824384 | bytes 1837056 | tf_op jit(solution)/shard_map/dot_general | solution.py:410
  92.4 0.9 slice_add_fusion
  93.3 2.1 reshape.127
  95.4 1.4 copy.30
  96.8 30.1 %all_to_all.10 = f32[16,192,33]{1,2,0:T(8,128)S(1)} all-to-all(f32[16,192,33]{1,2,0:T(8,128)S(1)} %copy.30), channel_id=1, replica_groups=mesh['gene'=8,'bin'=16] {'bin'}, dimensions={0} | all-to-all | bytes 811008 | tf_op jit(solution)/shard_map/all_to_all | solution.py:412
  126.9 1.0 copy.31
  127.9 2.1 reshape.128
  129.9 0.9 slice_multiply_fusion.1
  130.8 6.2 %reduce-scatter.2.cloned.1.call-done = f32[1,32,3328]{2,1,0:T(8,128)} async-done(((f32[8,32,3328]{2,1,0:T(8,128)}), f32[1,32,3328]{2,1,0:T(8,128)}) %reduce-scatter.2.cloned.1.call-update) | async-done | bytes 426000 | tf_op jit(solution)/shard_map/reduce_scatter | solution.py:431
  137.1 4.8 %fusion.6.x_ref = f32[32,3072]{1,0:T(8,128)} fusion(f32[3072,256]{1,0:T(8,128)S(1)} %copy-done, f32[3072,33]{0,1:T(8,128)} %reshape.128, f32[32,3328]{1,0:T(8,128)} %bitcast.88, f32[3072,32]{0,1:T(8,128)S(1)} %copy.34, f32[3072]{0:T(1024)S(1)} %bitcast.82), kind=kOutput, calls=%fused_computation.8 | convolution fusion | flops 302579712 | bytes 4763648 | tf_op jit(solution)/shard_map/dot_general | solution.py:440
  141.9 41.0 %shard_map.68 = f32[8,32,3072]{2,1,0:T(8,128)} custom-call(f32[32,3072]{1,0:T(8,128)} %fusion.6.x_ref), custom_call_target="tpu_custom_call" | custom-call | tf_op jit(solution)/shard_map/pallas_call | solution.py:250
  182.9 3.3 %convert_element_type.40 = bf16[8,32,3072]{2,1,0:T(8,128)(2,1)} convert(f32[8,32,3072]{2,1,0:T(8,128)} %shard_map.68) | non-fusion elementwise | flops 786432 | bytes 4718592 | tf_op jit(solution)/shard_map/convert_element_type | solution.py:446
  186.1 3.5 %copy.32 = f32[256,3072]{0,1:T(8,128)} copy(f32[256,3072]{1,0:T(8,128)} %bitcast.73) | data formatting | bytes 6291456 | tf_op jit(solution)/shard_map/reshape | solution.py:444
  189.7 10.8 %fusion.4.cross_ref = f32[16,16,2304]{2,1,0:T(8,128)} fusion(bf16[16,16,3072]{2,1,0:T(8,128)(2,1)} %bitcast.74, bf16[3072,2304]{1,0:T(8,128)(2,1)} %param.5), kind=kOutput, calls=%fused_computation.5 | convolution fusion | flops 3623878656 | bytes 18087936 | tf_op jit(solution)/shard_map/dot_general | solution.py:447
  200.5 1.3 fusion.45.gram_ref
  201.8 69.2 %shard_map.69 = f32[16,16,2304]{2,1,0:T(8,128)} custom-call(f32[16,16,2304]{2,1,0:T(8,128)} %fusion.4.cross_ref, f32[16,16,256]{2,1,0:T(8,128)} %fusion.45.gram_ref, f32[256,2304]{1,0:T(8,128)} %load_ref.1), custom_call_target="tpu_custom_call" | custom-call | tf_op jit(solution)/shard_map/pallas_call | solution.py:349
  271.0 3.2 %copy.45 = f32[256,2304]{1,0:T(8,128)} copy(f32[256,2304]{1,0:T(8,128)} %bitcast.78) | data formatting | bytes 4718592
  (15 shorter events, 0.1 us)
Async XLA Ops:
  7.2 1.9 copy-start
  15.8 38.1 %all-to-all-start = ((f32[16,192,33]{1,2,0:T(8,128)}), f32[16,192,33]{1,2,0:T(8,128)}, u32[]{:S(2)}, u32[]{:S(2)}) async-start(f32[16,192,33]{1,2,0:T(8,128)} %copy.26), calls=%async_computation.1 | async-start | bytes 1310720 | tf_op jit(solution)/shard_map/all_to_all | solution.py:386
  25.1 111.9 %reduce-scatter.2.cloned.1.call-start = ((), (), s32[]{:S(2)}) async-start(), calls=%async_computation.3 | async-start | bytes 3833856 | tf_op jit(solution)/shard_map/reduce_scatter | solution.py:431
  25.2 11.5 %copy-start.2 = (f32[256,2304]{1,0:T(8,128)S(1)}, f32[256,2304]{1,0:T(8,128)}, u32[]{:S(2)}) copy-start(f32[256,2304]{1,0:T(8,128)} %load_ref.1) | copy-start | bytes 7077892
  26.0 2.7 copy-start.3
  26.7 25.8 %collective-permute-start.2 = (f32[256]{0:T(256)}, f32[256]{0:T(256)}, u32[]{:S(2)}, u32[]{:S(2)}) collective-permute-start(f32[256]{0:T(256)} %bitcast.7), channel_id=1, source_target_pairs={{1,0},{2,1},{3,2},{4,3},{5,4},{6,5},{7,6},{8,7},{9,8},{10,9},{11,1... | collective-permute-start | bytes 3080 | tf_op jit(solution)/shard_map/ppermute | solution.py:17
  28.7 23.7 %collective-permute-start.3 = (f32[256]{0:T(256)}, f32[256]{0:T(256)}, u32[]{:S(2)}, u32[]{:S(2)}) collective-permute-start(f32[256]{0:T(256)} %bitcast.9), channel_id=1, source_target_pairs={{0,1},{1,2},{2,3},{3,4},{4,5},{5,6},{6,7},{7,8},{8,9},{9,10},{10,1... | collective-permute-start | bytes 3080 | tf_op jit(solution)/shard_map/ppermute | solution.py:17
  59.0 8.6 %copy-start.5 = (s32[3072,1]{0,1:T(1,128)}, s32[3072,1]{0,1:T(1,128)S(1)}, u32[]{:S(2)}) copy-start(s32[3072,1]{0,1:T(1,128)S(1)} %fusion.35) | copy-start | bytes 36868
  67.6 2.7 copy-start.4
  71.5 7.6 %collective-permute-start = (f32[256,32]{0,1:T(8,128)S(1)}, f32[256,32]{0,1:T(8,128)S(1)}, u32[]{:S(2)}, u32[]{:S(2)}) collective-permute-start(f32[256,32]{0,1:T(8,128)S(1)} %bitcast.84), channel_id=1, source_target_pairs={{1,0},{2,1},{3,2},{4,3},{5,4},{6,5},{7,6},{8,7},{9,8},{10,9},{11,1... | collective-permute-start | bytes 98312 | tf_op jit(solution)/shard_map/ppermute | solution.py:17
  73.4 6.9 %collective-permute-start.1 = (f32[256,32]{0,1:T(8,128)S(1)}, f32[256,32]{0,1:T(8,128)S(1)}, u32[]{:S(2)}, u32[]{:S(2)}) collective-permute-start(f32[256,32]{0,1:T(8,128)S(1)} %bitcast.85), channel_id=1, source_target_pairs={{0,1},{1,2},{2,3},{3,4},{4,5},{5,6},{6,7},{7,8},{8,9},{9,10},{10,1... | collective-permute-start | bytes 98312 | tf_op jit(solution)/shard_map/ppermute | solution.py:17
  80.6 3.7 %copy-start.6 = (s32[3072,1]{0,1:T(1,128)S(1)}, s32[3072,1]{0,1:T(1,128)}, u32[]{:S(2)}) copy-start(s32[3072,1]{0,1:T(1,128)} %copy-done.5) | copy-start | bytes 36868
  189.7 10.8 %copy-start.1 = (bf16[8,32,3072]{2,1,0:T(8,128)(2,1)S(1)}, bf16[8,32,3072]{2,1,0:T(8,128)(2,1)}, u32[]{:S(2)}) copy-start(bf16[8,32,3072]{2,1,0:T(8,128)(2,1)} %convert_element_type.40) | copy-start | bytes 4718596
Sparse Core Ops, SparseCore 0:
  51.3 85.7 reduce-scatter.1
where the time goes:
time: 282 us; the launch traced here: 281 us
  Pallas kernels  110 us (39%)
  matrix products  46.1 us (16%)
  local copies, waits for them, and re-layouts  31.5 us (11%)
  blocking collectives  30.1 us (11%)
  starting transfers between devices  23.6 us (8%)
  other arithmetic  17.9 us (6%)
  between operations  14.3 us (5%)
  waiting for transfers between devices  7.44 us (3%)
    pallas_call x1, Pallas kernels, loadings_update(): pl.pallas_call(functools.partial(loadings_kernel, count), out_shape=jax.S...  69.2 us
    pallas_call x1, Pallas kernels, exchange(): pl.pallas_call(functools.partial(exchange_kernel, axis, count, summed), o...  41 us
    all_to_all x1, blocking collectives, stencil_term(): lax.all_to_all(back_rows.reshape(bin_count, group_size, width + 1), 'bin'...  30.1 us
    ppermute x4, starting transfers between devices, passed_along(): return lax.ppermute(block, axis, route)  14.3 us
    dot_general x1, matrix products, on_device(): cross_part = jnp.dot(fac_bf_t, counts, preferred_element_type=jnp.float32)  10.8 us
    dot_general x1, matrix products, on_device(): lax.dot_general(load_bf, counts, right_dims, preferred_element_type=jnp.f...  10.7 us
    all_to_all x1, starting transfers between devices, stencil_term(): lax.all_to_all(payload.reshape(bin_count, group_size, width + 1), 'bin',...  9.29 us
    dot_general x1, matrix products, stencil_term(): jnp.dot(onehot, split_three(back), preferred_element_type=jnp.float32)  8.05 us
  transfers between devices with their start and end apart: 6, of which 2 were waited for; matrix products, arithmetic and copies ran while one was open for 21% of the time, Pallas kernels for 0%

commit v1 on v0

--- a/solution.py
+++ b/solution.py
@@ -428,11 +428,12 @@
     numer_part = lax.dot_general(load_bf, counts, right_dims, preferred_element_type=jnp.float32)
     gram_part = lax.dot_general(load_bf, load_bf, right_dims, preferred_element_type=jnp.float32)
     both = jnp.concatenate([numer_part, gram_part], 1)
+    own = lax.dynamic_slice_in_dim(factors, gene_at * width, width, 1)
+    both, own = lax.optimization_barrier((both, own))
     both = lax.psum_scatter(
         both.reshape(gene_count, width, -1), "gene", scatter_dimension=0, tiled=True
     ).reshape(width, -1)
     numer_t, gram_rows = both[:, :row_count], both[:, row_count:]
-    own = lax.dynamic_slice_in_dim(factors, gene_at * width, width, 1)
     smooth, degree = stencil_term(own, position, edge_codes)
     penalty = float(G * K) / 64.0
     own_t = own.T

time: 282 us -> 283 us (level)
    unnamed x21 -> x20, local copies, waits for them, and re-layouts: 7.68 us -> 5.47 us
  transfers between devices with their start and end apart: 6 -> 6, of which waited for: 2 -> 5; matrix products, arithmetic and copies ran while one was open for 21% -> 15% of each run, Pallas kernels for 0% -> 0%
where the time goes in v1:
time: 283 us; the launch traced here: 282 us
  Pallas kernels  110 us (39%)
  matrix products  46.9 us (17%)
  local copies, waits for them, and re-layouts  31.3 us (11%)
  blocking collectives  29.4 us (10%)
  starting transfers between devices  23.9 us (8%)
  other arithmetic  17.7 us (6%)
  between operations  14.3 us (5%)
  waiting for transfers between devices  8.09 us (3%)
    pallas_call x1, Pallas kernels, loadings_update(): pl.pallas_call(functools.partial(loadings_kernel, count), out_shape=jax.S...  69.2 us
    pallas_call x1, Pallas kernels, exchange(): pl.pallas_call(functools.partial(exchange_kernel, axis, count, summed), o...  41 us
    all_to_all x1, blocking collectives, stencil_term(): lax.all_to_all(back_rows.reshape(bin_count, group_size, width + 1), 'bin'...  29.4 us
    ppermute x4, starting transfers between devices, passed_along(): return lax.ppermute(block, axis, route)  14.5 us
    dot_general x1, matrix products, on_device(): cross_part = jnp.dot(fac_bf_t, counts, preferred_element_type=jnp.float32)  10.8 us
    dot_general x1, matrix products, on_device(): lax.dot_general(load_bf, counts, right_dims, preferred_element_type=jnp.f...  10.7 us
    all_to_all x1, starting transfers between devices, stencil_term(): lax.all_to_all(payload.reshape(bin_count, group_size, width + 1), 'bin',...  9.3 us
    dot_general x1, matrix products, stencil_term(): jnp.dot(onehot, split_three(back), preferred_element_type=jnp.float32)  8.05 us
  transfers between devices with their start and end apart: 6, of which 5 were waited for; matrix products, arithmetic and copies ran while one was open for 15% of the time, Pallas kernels for 0%

profile of v1, /device:TPU:1, one launch (start us, length us, event | category | flops | bytes accessed | tf_op | source)
XLA Modules:
  0.0 281.7 jit_solution(1215456991602248824)
XLA Ops:
  7.2 0.0 copy-start
  7.2 0.9 convert_element_type.37
  8.0 0.1 concatenate.56
  8.1 0.0 copy-start.2
  8.1 3.7 %fusion.17 = f32[256,256]{1,0:T(8,128)} fusion(f32[256,2304]{1,0:T(8,128)} %load_ref.1), kind=kOutput, calls=%fused_computation.25 | convolution fusion | flops 302579712 | bytes 2621440 | tf_op jit(solution)/shard_map/dot_general | solution.py:429
  11.9 10.7 %fusion.19 = f32[256,3072]{1,0:T(8,128)} fusion(bf16[3072,2304]{1,0:T(8,128)(2,1)} %param.5, f32[256,2304]{1,0:T(8,128)S(1)} %copy-done.2), kind=kOutput, calls=%fused_computation.27 | convolution fusion | flops 3624468480 | bytes 19660800 | tf_op jit(solution)/shard_map/dot_general | solution.py:428
  22.5 1.6 constant_dynamic-slice_fusion
  24.2 1.8 copy.35
  26.0 4.0 %pad_maximum_fusion = f32[256,3328]{1,0:T(8,128)} fusion(f32[256,256]{1,0:T(8,128)} %fusion.17, f32[256,3072]{1,0:T(8,128)} %fusion.19), kind=kLoop, calls=%fused_computation.9 | loop fusion | flops 851968 | bytes 6815744 | tf_op jit(solution)/shard_map/concatenate | solution.py:430
  30.0 1.0 concatenate.55
  31.0 1.3 copy.27
  32.4 0.9 pad_maximum_fusion.1
  33.2 9.3 %all-to-all-start = ((f32[16,192,33]{1,2,0:T(8,128)}), f32[16,192,33]{1,2,0:T(8,128)}, u32[]{:S(2)}, u32[]{:S(2)}) async-start(f32[16,192,33]{1,2,0:T(8,128)} %pad_maximum_fusion.1), calls=%async_computation.1 | async-start | bytes 1310720 | tf_op jit(solution)/shard_map/all_to_all | solution.py:386
  42.5 0.0 reduce-scatter.2.cloned.1.call-start
  42.6 0.7 fusion.38
  43.3 0.6 copy-done.3
  43.9 0.6 fusion.43
  44.5 2.0 collective-permute-start.2
  46.6 5.2 %collective-permute-start.3 = (f32[256]{0:T(256)}, f32[256]{0:T(256)}, u32[]{:S(2)}, u32[]{:S(2)}) collective-permute-start(f32[256]{0:T(256)} %bitcast.9), channel_id=1, source_target_pairs={{0,1},{1,2},{2,3},{3,4},{4,5},{5,6},{6,7},{7,8},{8,9},{9,10},{10,1... | collective-permute-start | bytes 3080 | tf_op jit(solution)/shard_map/ppermute | solution.py:17
  51.8 0.0 reduce-scatter.2.cloned.1.call-update
  51.8 0.6 fusion.44
  52.4 0.7 fusion.42
  53.1 0.7 collective-permute-done.2
  53.7 0.0 collective-permute-done.3
  53.7 0.9 fusion.34
  54.6 0.6 copy.39
  55.2 0.1 all-to-all-done
  55.4 2.1 copy.28
  57.4 2.1 reshape.123
  59.5 0.9 fusion.35
  60.4 0.0 copy-start.5
  60.4 1.1 reduce-precision_convert_fusion.3
  61.5 7.5 %fusion.1 = f32[3072,96]{0,1:T(8,128)S(1)} fusion(s32[3072]{0:T(1024)S(1)} %bitcast.86, bf16[3072,32]{0,1:T(8,128)(2,1)S(1)} %get-tuple-element.16, bf16[3072,32]{0,1:T(8,128)(2,1)S(1)} %get-tuple-element.17, bf16[3072,32]{0,1:T(8,128)(2,1)S(1)} %get-tuple-element.15), kind=kOutput, calls=%fused_computation.2 | convolution fusion | flops 1823145984 | bytes 1781760 | tf_op jit(solution)/shard_map/dot_general | solution.py:392
  69.0 0.8 slice_add_fusion.2
  69.8 1.9 reshape.124
  71.7 1.1 broadcast_multiply_fusion
  72.9 3.1 %collective-permute-start = (f32[256,32]{0,1:T(8,128)S(1)}, f32[256,32]{0,1:T(8,128)S(1)}, u32[]{:S(2)}, u32[]{:S(2)}) collective-permute-start(f32[256,32]{0,1:T(8,128)S(1)} %bitcast.84), channel_id=1, source_target_pairs={{1,0},{2,1},{3,2},{4,3},{5,4},{6,5},{7,6},{8,7},{9,8},{10,9},{11,1... | collective-permute-start | bytes 98312 | tf_op jit(solution)/shard_map/ppermute | solution.py:17
  76.0 4.2 %collective-permute-start.1 = (f32[256,32]{0,1:T(8,128)S(1)}, f32[256,32]{0,1:T(8,128)S(1)}, u32[]{:S(2)}, u32[]{:S(2)}) collective-permute-start(f32[256,32]{0,1:T(8,128)S(1)} %bitcast.85), channel_id=1, source_target_pairs={{0,1},{1,2},{2,3},{3,4},{4,5},{5,6},{6,7},{7,8},{8,9},{9,10},{10,1... | collective-permute-start | bytes 98312 | tf_op jit(solution)/shard_map/ppermute | solution.py:17
  80.2 0.1 fusion.41
  80.3 0.2 fusion.39
  80.5 0.4 collective-permute-done
  80.9 0.8 collective-permute-done.1
  81.7 0.3 fusion.23
  82.0 0.2 copy.38
  82.3 0.8 constant_dynamic-update-slice_fusion
  83.0 1.6 dynamic-update-slice.1
  84.6 1.1 reduce-precision_convert_fusion.1
  85.8 8.1 %fusion = f32[3072,99]{0,1:T(8,128)S(1)} fusion(s32[3072]{0:T(1024)S(1)} %bitcast.87, bf16[3072,33]{0,1:T(8,128)(2,1)S(1)} %get-tuple-element.13, bf16[3072,33]{0,1:T(8,128)(2,1)S(1)} %get-tuple-element.14, bf16[3072,33]{0,1:T(8,128)(2,1)S(1)} %get-tuple-element.12), kind=kOutput, calls=%fused_computation.1 | convolution fusion | flops 1879824384 | bytes 1837056 | tf_op jit(solution)/shard_map/dot_general | solution.py:410
  93.8 0.9 slice_add_fusion
  94.7 2.1 reshape.127
  96.8 1.4 copy.31
  98.2 29.4 %all_to_all.10 = f32[16,192,33]{1,2,0:T(8,128)S(1)} all-to-all(f32[16,192,33]{1,2,0:T(8,128)S(1)} %copy.31), channel_id=1, replica_groups=mesh['gene'=8,'bin'=16] {'bin'}, dimensions={0} | all-to-all | bytes 811008 | tf_op jit(solution)/shard_map/all_to_all | solution.py:412
  127.6 1.0 copy.32
  128.6 2.1 reshape.128
  130.6 0.9 slice_multiply_fusion.1
  131.5 6.1 %reduce-scatter.2.cloned.1.call-done = f32[1,32,3328]{2,1,0:T(8,128)} async-done(((f32[8,32,3328]{2,1,0:T(8,128)}), f32[1,32,3328]{2,1,0:T(8,128)}) %reduce-scatter.2.cloned.1.call-update) | async-done | bytes 426000 | tf_op jit(solution)/shard_map/reduce_scatter | solution.py:433
  137.7 4.8 %fusion.6.x_ref = f32[32,3072]{1,0:T(8,128)} fusion(f32[3072,256]{1,0:T(8,128)S(1)} %copy-done, f32[3072,33]{0,1:T(8,128)} %reshape.128, f32[32,3328]{1,0:T(8,128)} %bitcast.88, f32[3072,32]{0,1:T(8,128)S(1)} %copy.35, f32[3072]{0:T(1024)S(1)} %bitcast.82), kind=kOutput, calls=%fused_computation.8 | convolution fusion | flops 302579712 | bytes 4763648 | tf_op jit(solution)/shard_map/dot_general | solution.py:441
  142.5 41.0 %shard_map.68 = f32[8,32,3072]{2,1,0:T(8,128)} custom-call(f32[32,3072]{1,0:T(8,128)} %fusion.6.x_ref), custom_call_target="tpu_custom_call" | custom-call | tf_op jit(solution)/shard_map/pallas_call | solution.py:250
  183.5 3.3 %convert_element_type.40 = bf16[8,32,3072]{2,1,0:T(8,128)(2,1)} convert(f32[8,32,3072]{2,1,0:T(8,128)} %shard_map.68) | non-fusion elementwise | flops 786432 | bytes 4718592 | tf_op jit(solution)/shard_map/convert_element_type | solution.py:447
  186.7 3.5 %copy.33 = f32[256,3072]{0,1:T(8,128)} copy(f32[256,3072]{1,0:T(8,128)} %bitcast.73) | data formatting | bytes 6291456 | tf_op jit(solution)/shard_map/reshape | solution.py:445
  190.3 10.8 %fusion.4.cross_ref = f32[16,16,2304]{2,1,0:T(8,128)} fusion(bf16[16,16,3072]{2,1,0:T(8,128)(2,1)} %bitcast.74, bf16[3072,2304]{1,0:T(8,128)(2,1)} %param.5), kind=kOutput, calls=%fused_computation.5 | convolution fusion | flops 3623878656 | bytes 18087936 | tf_op jit(solution)/shard_map/dot_general | solution.py:448
  201.1 1.3 fusion.45.gram_ref
  202.4 69.2 %shard_map.69 = f32[16,16,2304]{2,1,0:T(8,128)} custom-call(f32[16,16,2304]{2,1,0:T(8,128)} %fusion.4.cross_ref, f32[16,16,256]{2,1,0:T(8,128)} %fusion.45.gram_ref, f32[256,2304]{1,0:T(8,128)} %load_ref.1), custom_call_target="tpu_custom_call" | custom-call | tf_op jit(solution)/shard_map/pallas_call | solution.py:349
  271.6 3.2 %copy.46 = f32[256,2304]{1,0:T(8,128)} copy(f32[256,2304]{1,0:T(8,128)} %bitcast.78) | data formatting | bytes 4718592
  (15 shorter events, 0.1 us)
Async XLA Ops:
  7.2 15.4 %copy-start = (f32[3072,256]{1,0:T(8,128)S(1)}, f32[3072,256]{1,0:T(8,128)}, u32[]{:S(2)}) copy-start(f32[3072,256]{1,0:T(8,128)} %param.6) | copy-start | bytes 9437188
  8.1 3.8 %copy-start.2 = (f32[256,2304]{1,0:T(8,128)S(1)}, f32[256,2304]{1,0:T(8,128)}, u32[]{:S(2)}) copy-start(f32[256,2304]{1,0:T(8,128)} %load_ref.1) | copy-start | bytes 7077892
  33.2 22.1 %all-to-all-start = ((f32[16,192,33]{1,2,0:T(8,128)}), f32[16,192,33]{1,2,0:T(8,128)}, u32[]{:S(2)}, u32[]{:S(2)}) async-start(f32[16,192,33]{1,2,0:T(8,128)} %pad_maximum_fusion.1), calls=%async_computation.1 | async-start | bytes 1310720 | tf_op jit(solution)/shard_map/all_to_all | solution.py:386
  42.5 95.1 %reduce-scatter.2.cloned.1.call-start = ((), (), s32[]{:S(2)}) async-start(), calls=%async_computation.3 | async-start | bytes 3833856 | tf_op jit(solution)/shard_map/reduce_scatter | solution.py:433
  43.3 0.6 copy-start.3
  44.5 9.2 %collective-permute-start.2 = (f32[256]{0:T(256)}, f32[256]{0:T(256)}, u32[]{:S(2)}, u32[]{:S(2)}) collective-permute-start(f32[256]{0:T(256)} %bitcast.7), channel_id=1, source_target_pairs={{1,0},{2,1},{3,2},{4,3},{5,4},{6,5},{7,6},{8,7},{9,8},{10,9},{11,1... | collective-permute-start | bytes 3080 | tf_op jit(solution)/shard_map/ppermute | solution.py:17
  46.6 7.2 %collective-permute-start.3 = (f32[256]{0:T(256)}, f32[256]{0:T(256)}, u32[]{:S(2)}, u32[]{:S(2)}) collective-permute-start(f32[256]{0:T(256)} %bitcast.9), channel_id=1, source_target_pairs={{0,1},{1,2},{2,3},{3,4},{4,5},{5,6},{6,7},{7,8},{8,9},{9,10},{10,1... | collective-permute-start | bytes 3080 | tf_op jit(solution)/shard_map/ppermute | solution.py:17
  60.4 8.6 %copy-start.5 = (s32[3072,1]{0,1:T(1,128)}, s32[3072,1]{0,1:T(1,128)S(1)}, u32[]{:S(2)}) copy-start(s32[3072,1]{0,1:T(1,128)S(1)} %fusion.35) | copy-start | bytes 36868
  69.0 2.7 copy-start.4
  72.9 8.0 %collective-permute-start = (f32[256,32]{0,1:T(8,128)S(1)}, f32[256,32]{0,1:T(8,128)S(1)}, u32[]{:S(2)}, u32[]{:S(2)}) collective-permute-start(f32[256,32]{0,1:T(8,128)S(1)} %bitcast.84), channel_id=1, source_target_pairs={{1,0},{2,1},{3,2},{4,3},{5,4},{6,5},{7,6},{8,7},{9,8},{10,9},{11,1... | collective-permute-start | bytes 98312 | tf_op jit(solution)/shard_map/ppermute | solution.py:17
  76.0 5.7 %collective-permute-start.1 = (f32[256,32]{0,1:T(8,128)S(1)}, f32[256,32]{0,1:T(8,128)S(1)}, u32[]{:S(2)}, u32[]{:S(2)}) collective-permute-start(f32[256,32]{0,1:T(8,128)S(1)} %bitcast.85), channel_id=1, source_target_pairs={{0,1},{1,2},{2,3},{3,4},{4,5},{5,6},{6,7},{7,8},{8,9},{9,10},{10,1... | collective-permute-start | bytes 98312 | tf_op jit(solution)/shard_map/ppermute | solution.py:17
  82.0 3.7 %copy-start.6 = (s32[3072,1]{0,1:T(1,128)S(1)}, s32[3072,1]{0,1:T(1,128)}, u32[]{:S(2)}) copy-start(s32[3072,1]{0,1:T(1,128)} %copy-done.5) | copy-start | bytes 36868
  190.3 10.8 %copy-start.1 = (bf16[8,32,3072]{2,1,0:T(8,128)(2,1)S(1)}, bf16[8,32,3072]{2,1,0:T(8,128)(2,1)}, u32[]{:S(2)}) copy-start(bf16[8,32,3072]{2,1,0:T(8,128)(2,1)} %convert_element_type.40) | copy-start | bytes 4718596
Sparse Core Ops, SparseCore 0:
  51.9 85.7 reduce-scatter.1
